TPU v7x, 32 devices: a whole 2x2x4 slice. The times are simulated.
32 devices in a mesh: layer: 4 (over y, x), feat: 8 (over z, core).
Axes of the slice: x: 2, y: 2, z: 4, core: 2. Of those that a mesh axis runs over, the one named last changes fastest.
Arguments:
- acts: bfloat16 [4, 256, 8192], P(None, 'layer', 'feat'), may hold values from -6 to 6
- layer_order: int32 [4, 4], P('layer'), may hold values from 0 to 3, each once within a row
- groups: int32 [8192], P('feat'), may hold values from 0 to 63
- group_scale: float32 [4, 64], P('layer'), may hold values from 0.25 to 4
- shrink: float32 [4], P('layer'), may hold values from 0.1 to 0.6
Outputs:
- factor_tiles: float32 [4, 8, 4, 1024, 1024], P('layer', 'feat')
- far_tiles: float32 [4, 8, 512, 1024], P('layer', 'feat')
Inputs may be any that keep to these rules, and one draw needn't show every extreme that they name: Each row of layer_order names every layer once.
All inputs are finite; a program needn't handle non-finite values.
Results may differ from a plain program's by a relative error of at most 0.0003.
Values may be sent and summed in bfloat16 or wider, within the bound.
No kernel may reach another device: no remote copies, remote signals or barrier semaphores. Data moves between devices by JAX's collectives and lax.ppermute only.
A program may use at most 64 MiB of HBM per device.

v0:
```python
import math

import jax
import jax.numpy as jnp
from jax import lax
from jax.experimental import pallas as pl
from jax.experimental.pallas import tpu as pltpu
from jax.sharding import PartitionSpec as P

TRANSPOSED = (((0,), (0,)), ((), ()))
SMEM = pl.BlockSpec(memory_space=pltpu.SMEM)
VMEM = pl.BlockSpec(memory_space=pltpu.VMEM)
HBM = pl.BlockSpec(memory_space=pltpu.HBM)
ANY = pl.BlockSpec(memory_space=pl.ANY)


def room(*shapes):
    total = sum(math.prod(shape) * jnp.dtype(dtype).itemsize for shape, dtype in shapes)
    return pltpu.CompilerParams(vmem_limit_bytes=total + (2 << 20))


def like(*arrays):
    return [(a.shape, a.dtype) for a in arrays]


def partner(i, k, count):
    return (i + k) % count if count & (count - 1) else i ^ k


def select(acts, layer_order):
    layers, rows, width = acts.shape

    def body(order_ref, acts_ref, *rest):
        outs, (held, order, sem) = rest[:layers], rest[layers:]
        copies = [
            pltpu.make_async_copy(order_ref, order, sem.at[0]),
            pltpu.make_async_copy(acts_ref, held, sem.at[1]),
        ]
        for copy in copies:
            copy.start()
        here = lax.axis_index("layer")
        copies[0].wait()
        slots = []
        for k in range(layers):
            layer = partner(here, k, layers)
            slot = jnp.int32(0)
            for s in range(1, layers):
                slot = jnp.where(order[0, s] == layer, s, slot)
            slots.append(slot)
        copies[1].wait()
        for out, slot in zip(outs, slots):
            out[...] = held[slot]

    return pl.pallas_call(
        body,
        out_shape=[jax.ShapeDtypeStruct((rows, width), acts.dtype)] * layers,
        in_specs=[ANY, ANY],
        out_specs=[VMEM] * layers,
        scratch_shapes=[
            pltpu.VMEM(acts.shape, acts.dtype),
            pltpu.SMEM(layer_order.shape, layer_order.dtype),
            pltpu.SemaphoreType.DMA((2,)),
        ],
        name="select",
    )(layer_order, acts)


def prepare(block, groups, group_scale):
    count = group_scale.shape[1]

    def body(scale_ref, groups_ref, block_ref, out_ref, gains_ref):
        out_ref[...] = block_ref[...]
        line = jnp.zeros(groups_ref.shape, jnp.float32)
        for g in range(count):
            line = jnp.where(groups_ref[...] == g, scale_ref[0, g], line)
        gains_ref[...] = line

    return pl.pallas_call(
        body,
        out_shape=[
            jax.ShapeDtypeStruct(block.shape, block.dtype),
            jax.ShapeDtypeStruct((1, groups.shape[0]), jnp.float32),
        ],
        in_specs=[SMEM, VMEM, VMEM],
        out_specs=[VMEM] * 2,
        compiler_params=room(*like(block, block, groups, groups)),
        name="prepare",
    )(group_scale, groups[None], block)


def join(blocks):
    if len(blocks) == 1:
        return blocks[0]
    shape = (sum(b.shape[0] for b in blocks), blocks[0].shape[1])

    def body(*refs):
        assemble(refs[-1], refs[:-1])

    return pl.pallas_call(
        body,
        out_shape=jax.ShapeDtypeStruct(shape, blocks[0].dtype),
        in_specs=[VMEM] * len(blocks),
        out_specs=VMEM,
        compiler_params=room(*like(*blocks) * 2),
        name="join",
    )(*blocks)


def gather(blocks):
    rows, width = blocks[0].shape
    tokens = rows * len(blocks)

    def body(*refs):
        parts, (own_ref, part_ref) = refs[:-2], refs[-2:]
        total = jnp.zeros((1, width), jnp.float32)
        for j, part in enumerate(parts):
            own_ref[j * rows : (j + 1) * rows, :] = part[...]
            value = part[...].astype(jnp.float32)
            total = total + jnp.sum(value * value, axis=0, keepdims=True)
        part_ref[...] = jnp.broadcast_to(jnp.sum(total) / tokens, part_ref.shape)

    return pl.pallas_call(
        body,
        out_shape=[
            jax.ShapeDtypeStruct((tokens, width), blocks[0].dtype),
            jax.ShapeDtypeStruct((8, 128), jnp.float32),
        ],
        in_specs=[VMEM] * len(blocks),
        out_specs=[VMEM] * 2,
        compiler_params=room(*like(*blocks) * 2),
        name="gather",
    )(*blocks)


def place():
    f = lax.axis_index("feat")
    return f, f // 2, f % 2


def assemble(panel_ref, blocks):
    start = 0
    for block in blocks:
        panel_ref[start : start + block.shape[0], :] = block[...]
        start += block.shape[0]


def tile(stack, count, own, blocks, index, shrink, keep=False, diagonal=None, odd=()):
    tokens, width = own.shape
    step = next(s for s in (128, 64, 32, 16, 8, width) if width % s == 0)
    steps = width // step
    extra = [] if diagonal is None else diagonal
    given = [*blocks, *odd]

    def body(shrink_ref, own_ref, *rest):
        parts, rest = rest[: len(given)], rest[len(given) :]
        added, rest = rest[: len(extra)], rest[len(extra) :]
        rest = rest[(stack is not None) :]
        out_ref, rest = rest[0], rest[1:]
        if keep:
            panel, rest = rest[0], rest[1:]
        else:
            panel, rest = rest[-1], rest[:-1]
        buffer, sem = rest
        _, _, core = place()
        to = index(core)
        if odd:
            pl.when(core == 0)(lambda: assemble(panel, parts[: len(blocks)]))
            pl.when(core != 0)(lambda: assemble(panel, parts[len(blocks) :]))
        else:
            assemble(panel, parts)
        scale = (1.0 - shrink_ref[0]) * (1.0 / tokens)
        if extra:
            gains_ref, sums = added[0], added[1:]
            trace = sums[0][0:1, 0:1]
            for other in sums[1:]:
                trace = trace + other[0:1, 0:1]
            mu = trace * (1.0 / (width * lax.axis_size("feat")))
            line = gains_ref[...] * (mu * shrink_ref[0])
        copies = []
        for i in range(steps):
            rows = slice(i * step, (i + 1) * step)
            value = (
                lax.dot_general(
                    own_ref[:, rows],
                    panel[...],
                    TRANSPOSED,
                    preferred_element_type=jnp.float32,
                )
                * scale
            )
            buffer[rows, :] = value
            if extra:
                shape = (step, step)
                same = lax.broadcasted_iota(jnp.int32, shape, 0) == lax.broadcasted_iota(
                    jnp.int32, shape, 1
                )
                buffer[rows, rows] = value[:, rows] + jnp.where(same, line[:, rows], 0.0)
            copies.append(
                pltpu.make_async_copy(buffer.at[rows, :], out_ref.at[to, rows, :], sem.at[i])
            )
            copies[-1].start()
        for copy in copies:
            copy.wait()

    out_shape = [jax.ShapeDtypeStruct((count, width, width), jnp.float32)]
    out_specs = [ANY]
    scratch = [pltpu.VMEM((width, width), jnp.float32), pltpu.SemaphoreType.DMA((steps,))]
    if keep:
        out_shape.append(jax.ShapeDtypeStruct((tokens, width), own.dtype))
        out_specs.append(VMEM)
    else:
        scratch.append(pltpu.VMEM((tokens, width), own.dtype))
    operands = [shrink, own, *given, *extra] + ([] if stack is None else [stack])
    in_specs = [SMEM] + [VMEM] * (1 + len(given) + len(extra)) + [ANY] * (stack is not None)
    outs = pl.pallas_call(
        body,
        out_shape=out_shape,
        in_specs=in_specs,
        out_specs=out_specs,
        scratch_shapes=scratch,
        input_output_aliases={} if stack is None else {len(operands) - 1: 0},
        compiler_params=room(*like(own, own, *given, *extra), ((width, width), jnp.float32)),
        cost_estimate=pl.CostEstimate(
            flops=2 * tokens * width * width,
            bytes_accessed=4 * width * width + 4 * tokens * width,
            transcendentals=0,
        ),
        name="gram_tile",
    )(*operands)
    return outs if keep else outs[0]


def far_tile(own, blocks, shrink):
    tokens, width = own.shape
    rows = width // 2

    step = next(s for s in (128, 64, 32, 16, 8, rows) if rows % s == 0)
    steps = rows // step

    def body(shrink_ref, own_ref, *rest):
        parts, (out_ref, left, panel, buffer, sem) = rest[: len(blocks)], rest[len(blocks) :]
        f, _, _ = place()
        lower = f < lax.axis_size("feat") // 2
        scale = (1.0 - shrink_ref[0]) * (1.0 / tokens)
        assemble(panel, parts)

        @pl.when(lower)
        def _():
            left[...] = own_ref[:, :rows]

        @pl.when(jnp.logical_not(lower))
        def _():
            left[...] = panel[:, rows:]
            panel[...] = own_ref[...]

        copies = []
        for i in range(steps):
            part = slice(i * step, (i + 1) * step)
            buffer[part, :] = (
                lax.dot_general(
                    left[:, part],
                    panel[...],
                    TRANSPOSED,
                    preferred_element_type=jnp.float32,
                )
                * scale
            )
            copies.append(
                pltpu.make_async_copy(buffer.at[part, :], out_ref.at[part, :], sem.at[i])
            )
            copies[-1].start()
        for copy in copies:
            copy.wait()

    return pl.pallas_call(
        body,
        out_shape=jax.ShapeDtypeStruct((rows, width), jnp.float32),
        in_specs=[SMEM] + [VMEM] * (1 + len(blocks)),
        out_specs=ANY,
        scratch_shapes=[
            pltpu.VMEM((tokens, rows), own.dtype),
            pltpu.VMEM((tokens, width), own.dtype),
            pltpu.VMEM((rows, width), jnp.float32),
            pltpu.SemaphoreType.DMA((steps,)),
        ],
        compiler_params=room(*like(own, own, own, *blocks), ((width, width), jnp.float32)),
        cost_estimate=pl.CostEstimate(
            flops=2 * tokens * rows * width,
            bytes_accessed=4 * rows * width + 4 * tokens * width,
            transcendentals=0,
        ),
        name="far_tile",
    )(shrink, own, *blocks)


def behind(block, k):
    count = lax.axis_size("feat")
    return lax.ppermute(block, "feat", [((i + 2 * k) % count, i) for i in range(count)])


def swapped(block):
    return lax.ppermute(block, "feat", [(i, i ^ 1) for i in range(lax.axis_size("feat"))])


def shards(acts, layer_order, groups, group_scale, shrink):
    layers, _, _ = acts.shape
    half = lax.axis_size("feat") // 2
    chips = half
    reach = chips // 2

    sent = select(acts, layer_order)
    blocks = [sent[0]]
    for k in range(1, layers):
        route = [(i, partner(i, k, layers)) for i in range(layers)]
        blocks.append(lax.ppermute(sent[k], "layer", route))

    parts = [join(blocks[:1]), join(blocks[1:-1]), join(blocks[-1:])]
    ahead = [parts]
    for k in range(1, reach + 1):
        if k == 2:
            parts = [join(parts[:-1]), parts[-1]]
        moved = []
        for block in parts:
            moved.append(behind(block, 1))
        parts = moved
        ahead.append(parts)

    first, gains = prepare(blocks[0], groups, group_scale)
    own, part = gather([first, *blocks[1:]])
    part = part + swapped(part)
    sums = [part]
    for k in range(1, chips):
        sums.append(behind(part, k))
    stack = None
    for k in range(1, reach):
        stack, panel = tile(stack, half, own, ahead[k], lambda core, k=k: 2 * k, shrink, keep=True)
        other = swapped(panel)
        if k == reach - 1:
            stack = tile(stack, half, own, [own], lambda core: 0, shrink, diagonal=[gains, *sums])
        index = lambda core, k=k: jnp.where(core == 0, 2 * k + 1, 2 * k - 1)
        stack = tile(stack, half, own, [other], index, shrink)
    other = swapped(own)
    odd = []
    for block in ahead[reach]:
        odd.append(swapped(block))
    far = far_tile(own, ahead[reach], shrink)
    index = lambda core: jnp.where(core == 0, 1, half - 1)
    stack = tile(stack, half, own, [other], index, shrink, odd=odd)
    return (stack[None, None], far[None, None])


def solution(mesh):
    placed = (P(None, "layer", "feat"), P("layer", None), P("feat"), P("layer", None), P("layer"))

    return jax.shard_map(
        shards,
        mesh=mesh,
        in_specs=placed,
        out_specs=(P("layer", "feat", None, None, None), P("layer", "feat", None, None)),
        check_vma=False,
    )
```

profile of v0, /device:TPU:0, one launch (start us, length us, event | category | flops | bytes accessed | tf_op | source)
XLA Modules:
  0.0 66.0 jit_solution(12392048148488541134)
XLA Ops:
  0.6 1.9 %select.1 = (bf16[64,1024]{1,0:T(8,128)(2,1)}, bf16[64,1024]{1,0:T(8,128)(2,1)}, bf16[64,1024]{1,0:T(8,128)(2,1)}, bf16[64,1024]{1,0:T(8,128)(2,1)}) custom-call(s32[1,4]{1,0:T(1,128)} %order_ref.1, bf16[4,64,1024]{2,1,0:T(8,128)(2,1)} %acts_ref.1), custom_call_target="tpu_custom_call" | custom-call | tf_op jit(solution)/shard_map/select/pallas_call | solution.py:54
  2.5 3.0 %collective-permute-start = (bf16[64,1024]{1,0:T(8,128)(2,1)}, bf16[64,1024]{1,0:T(8,128)(2,1)S(1)}, u32[]{:S(2)}, u32[]{:S(2)}) collective-permute-start(bf16[64,1024]{1,0:T(8,128)(2,1)} %get-tuple-element.14), channel_id=1, source_target_pairs={{0,8},{8,0},{16,24},{24,16},{1,9},{9,1},{17,25},{25,17},{2,10},{10... | collective-permute-start | bytes 393224 | tf_op jit(solution)/shard_map/ppermute | solution.py:315
  5.5 1.5 %collective-permute-start.1 = (bf16[64,1024]{1,0:T(8,128)(2,1)}, bf16[64,1024]{1,0:T(8,128)(2,1)S(1)}, u32[]{:S(2)}, u32[]{:S(2)}) collective-permute-start(bf16[64,1024]{1,0:T(8,128)(2,1)} %get-tuple-element.15), channel_id=1, source_target_pairs={{0,16},{8,24},{16,0},{24,8},{1,17},{9,25},{17,1},{25,9},{2,18},{10... | collective-permute-start | bytes 393224 | tf_op jit(solution)/shard_map/ppermute | solution.py:315
  7.1 2.2 %collective-permute-done.refs_1_.refs_0_ = bf16[64,1024]{1,0:T(8,128)(2,1)S(1)} collective-permute-done((bf16[64,1024]{1,0:T(8,128)(2,1)}, bf16[64,1024]{1,0:T(8,128)(2,1)S(1)}, u32[]{:S(2)}, u32[]{:S(2)}) %collective-permute-start) | collective-permute-done | bytes 131104 | tf_op jit(solution)/shard_map/ppermute | solution.py:315
  9.2 1.5 %collective-permute-done.1.refs_2_.refs_1_ = bf16[64,1024]{1,0:T(8,128)(2,1)S(1)} collective-permute-done((bf16[64,1024]{1,0:T(8,128)(2,1)}, bf16[64,1024]{1,0:T(8,128)(2,1)S(1)}, u32[]{:S(2)}, u32[]{:S(2)}) %collective-permute-start.1) | collective-permute-done | bytes 131104 | tf_op jit(solution)/shard_map/ppermute | solution.py:315
  10.7 3.7 %collective-permute-start.5 = (bf16[128,1024]{1,0:T(8,128)(2,1)S(1)}, bf16[128,1024]{1,0:T(8,128)(2,1)S(1)}, u32[]{:S(2)}, u32[]{:S(2)}) collective-permute-start(bf16[128,1024]{1,0:T(8,128)(2,1)S(1)} %join.2), channel_id=1, source_target_pairs={{2,0},{3,1},{4,2},{5,3},{6,4},{7,5},{0,6},{1,7},{10,8},{11,9},{12,... | collective-permute-start | bytes 786440 | tf_op jit(solution)/shard_map/ppermute | solution.py:298
  14.4 0.4 collective-permute-start.4
  14.8 1.5 %collective-permute-start.2 = (bf16[64,1024]{1,0:T(8,128)(2,1)}, bf16[64,1024]{1,0:T(8,128)(2,1)S(1)}, u32[]{:S(2)}, u32[]{:S(2)}) collective-permute-start(bf16[64,1024]{1,0:T(8,128)(2,1)} %get-tuple-element.16), channel_id=1, source_target_pairs={{0,24},{8,16},{16,8},{24,0},{1,25},{9,17},{17,9},{25,1},{2,26},{10... | collective-permute-start | bytes 393224 | tf_op jit(solution)/shard_map/ppermute | solution.py:315
  16.3 5.4 %collective-permute-done.4.refs_0_.rest_0_ = bf16[64,1024]{1,0:T(8,128)(2,1)S(1)} collective-permute-done((bf16[64,1024]{1,0:T(8,128)(2,1)}, bf16[64,1024]{1,0:T(8,128)(2,1)S(1)}, u32[]{:S(2)}, u32[]{:S(2)}) %collective-permute-start.4) | collective-permute-done | bytes 131104 | tf_op jit(solution)/shard_map/ppermute | solution.py:298
  21.7 0.0 collective-permute-done.5.refs_1_.rest_1_
  21.8 4.2 %collective-permute-start.6 = (bf16[192,1024]{1,0:T(8,128)(2,1)S(1)}, bf16[192,1024]{1,0:T(8,128)(2,1)S(1)}, u32[]{:S(2)}, u32[]{:S(2)}) collective-permute-start(bf16[192,1024]{1,0:T(8,128)(2,1)S(1)} %join.3), channel_id=1, source_target_pairs={{2,0},{3,1},{4,2},{5,3},{6,4},{7,5},{0,6},{1,7},{10,8},{11,9},{12,... | collective-permute-start | bytes 1179656 | tf_op jit(solution)/shard_map/ppermute | solution.py:298
  26.0 0.0 collective-permute-done.2.refs_3_
  26.0 0.1 collective-permute-start.8
  26.7 0.0 copy-start
  26.7 0.9 %copy-done = bf16[64,1024]{1,0:T(8,128)(2,1)S(1)} copy-done((bf16[64,1024]{1,0:T(8,128)(2,1)S(1)}, bf16[64,1024]{1,0:T(8,128)(2,1)}, u32[]{:S(2)}) %copy-start) | copy-done | bytes 131096
  27.6 0.0 copy-start.1
  27.6 0.7 %copy-done.1 = s32[1024]{0:T(1024)S(1)} copy-done((s32[1024]{0:T(1024)S(1)}, s32[1024]{0:T(1024)}, u32[]{:S(2)}) %copy-start.1) | copy-done | bytes 4120
  28.3 0.0 copy-start.2
  28.3 0.7 copy-done.2
  29.0 0.6 prepare.1
  29.6 0.2 gather.1
  29.8 5.4 %collective-permute-done.8.rest_2_ = bf16[64,1024]{1,0:T(8,128)(2,1)S(1)} collective-permute-done((bf16[64,1024]{1,0:T(8,128)(2,1)S(1)}, bf16[64,1024]{1,0:T(8,128)(2,1)S(1)}, u32[]{:S(2)}, u32[]{:S(2)}) %collective-permute-start.8) | collective-permute-done | bytes 131104 | tf_op jit(solution)/shard_map/ppermute | solution.py:298
  35.2 2.4 %gram_tile.4 = (f32[4,1024,1024]{2,1,0:T(8,128)}, bf16[256,1024]{1,0:T(8,128)(2,1)S(1)}) custom-call(f32[1]{0:T(128)S(6)} %copy.13.shrink_ref, bf16[256,1024]{1,0:T(8,128)(2,1)S(1)} %get-tuple-element.17.own_ref.rest_0_, bf16[64,1024]{1,0:T(8,128)(2,1)S(1)} %collective-permute-done.4.refs_0_.rest_0_, ...), custom_call_target="tpu_custom_call" | custom-call | flops 536870912 | bytes 5242880 | tf_op jit(solution)/shard_map/gram_tile/pallas_call | solution.py:215
  37.6 0.1 collective-permute-start.11
  37.6 0.5 collective-permute-start.3
  38.1 0.0 collective-permute-done.6.rest_0_
  38.1 0.1 collective-permute-start.7
  38.2 4.3 %collective-permute-start.9 = (bf16[64,1024]{1,0:T(8,128)(2,1)S(1)}, bf16[64,1024]{1,0:T(8,128)(2,1)S(1)}, u32[]{:S(2)}, u32[]{:S(2)}) collective-permute-start(bf16[64,1024]{1,0:T(8,128)(2,1)S(1)} %collective-permute-done.8.rest_2_), channel_id=1, source_target_pairs={{2,0},{3,1},{4,2},{5,3},{6,4},{7,5},{0,6},{1,7},{10,8},{11,9},{12,... | collective-permute-start | bytes 393224 | tf_op jit(solution)/shard_map/ppermute | solution.py:298
  42.5 0.2 collective-permute-start.12
  42.7 1.0 %collective-permute-done.12 = f32[8,128]{1,0:T(8,128)S(1)} collective-permute-done((f32[8,128]{1,0:T(8,128)S(1)}, f32[8,128]{1,0:T(8,128)S(1)}, u32[]{:S(2)}, u32[]{:S(2)}) %collective-permute-start.12) | collective-permute-done | bytes 4128 | tf_op jit(solution)/shard_map/ppermute | solution.py:302
  43.7 1.5 %collective-permute-start.13 = (f32[8,128]{1,0:T(8,128)S(1)}, f32[8,128]{1,0:T(8,128)S(1)}, u32[]{:S(2)}, u32[]{:S(2)}) collective-permute-start(f32[8,128]{1,0:T(8,128)S(1)} %add.3.rest_2_), channel_id=1, source_target_pairs={{2,0},{3,1},{4,2},{5,3},{6,4},{7,5},{0,6},{1,7},{10,8},{11,9},{12,... | collective-permute-start | bytes 12296 | tf_op jit(solution)/shard_map/ppermute | solution.py:298
  45.1 2.1 %collective-permute-done.13.rest_3_ = f32[8,128]{1,0:T(8,128)S(1)} collective-permute-done((f32[8,128]{1,0:T(8,128)S(1)}, f32[8,128]{1,0:T(8,128)S(1)}, u32[]{:S(2)}, u32[]{:S(2)}) %collective-permute-start.13) | collective-permute-done | bytes 4128 | tf_op jit(solution)/shard_map/ppermute | solution.py:298
  47.3 0.0 collective-permute-start.14
  47.3 0.0 collective-permute-done.9.rest_1_
  47.3 0.0 collective-permute-start.10
  47.3 4.5 %collective-permute-done.14.rest_4_ = f32[8,128]{1,0:T(8,128)S(1)} collective-permute-done((f32[8,128]{1,0:T(8,128)S(1)}, f32[8,128]{1,0:T(8,128)S(1)}, u32[]{:S(2)}, u32[]{:S(2)}) %collective-permute-start.14) | collective-permute-done | bytes 4128 | tf_op jit(solution)/shard_map/ppermute | solution.py:298
  51.8 0.9 %collective-permute-start.15 = (f32[8,128]{1,0:T(8,128)S(1)}, f32[8,128]{1,0:T(8,128)S(1)}, u32[]{:S(2)}, u32[]{:S(2)}) collective-permute-start(f32[8,128]{1,0:T(8,128)S(1)} %add.3.rest_2_), channel_id=1, source_target_pairs={{6,0},{7,1},{0,2},{1,3},{2,4},{3,5},{4,6},{5,7},{14,8},{15,9},{8,1... | collective-permute-start | bytes 12296 | tf_op jit(solution)/shard_map/ppermute | solution.py:298
  52.7 4.5 %collective-permute-done.15.rest_5_ = f32[8,128]{1,0:T(8,128)S(1)} collective-permute-done((f32[8,128]{1,0:T(8,128)S(1)}, f32[8,128]{1,0:T(8,128)S(1)}, u32[]{:S(2)}, u32[]{:S(2)}) %collective-permute-start.15) | collective-permute-done | bytes 4128 | tf_op jit(solution)/shard_map/ppermute | solution.py:298
  57.2 2.3 %gram_tile.5.rest_1_ = f32[4,1024,1024]{2,1,0:T(8,128)} custom-call(f32[1]{0:T(128)S(6)} %copy.13.shrink_ref, bf16[256,1024]{1,0:T(8,128)(2,1)S(1)} %get-tuple-element.17.own_ref.rest_0_, bf16[256,1024]{1,0:T(8,128)(2,1)S(1)} %get-tuple-element.17.own_ref.rest_0_, f32[1,1024]{1,0:T(1,128)S(1)} %get-tuple-element.19.rest_1_, ...), custom_call_target="tpu_custom_call", output_to_operand_aliasing={{}: (8, {})} | custom-call | flops 536870912 | bytes 5242880 | tf_op jit(solution)/shard_map/gram_tile/pallas_call | solution.py:215
  59.6 1.7 %far_tile.1 = f32[512,1024]{1,0:T(8,128)} custom-call(f32[1]{0:T(128)S(6)} %copy.13.shrink_ref, bf16[256,1024]{1,0:T(8,128)(2,1)S(1)} %get-tuple-element.17.own_ref.rest_0_, bf16[192,1024]{1,0:T(8,128)(2,1)S(1)} %collective-permute-done.6.rest_0_, bf16[64,1024]{1,0:T(8,128)(2,1)S(1)} %collective-permute-done.9.rest_1_), custom_call_target="tpu_custom_call" | custom-call | flops 268435456 | bytes 3145728 | tf_op jit(solution)/shard_map/far_tile/pallas_call | solution.py:275
  61.2 0.0 collective-permute-done.11.rest_0_
  61.2 2.3 %gram_tile.6.rest_3_ = f32[4,1024,1024]{2,1,0:T(8,128)} custom-call(f32[1]{0:T(128)S(6)} %copy.13.shrink_ref, bf16[256,1024]{1,0:T(8,128)(2,1)S(1)} %get-tuple-element.17.own_ref.rest_0_, bf16[256,1024]{1,0:T(8,128)(2,1)S(1)} %collective-permute-done.11.rest_0_, f32[4,1024,1024]{2,1,0:T(8,128)} %gram_tile.5.rest_1_), custom_call_target="tpu_custom_call", output_to_operand_aliasing={{}: (3, {})} | custom-call | flops 536870912 | bytes 5242880 | tf_op jit(solution)/shard_map/gram_tile/pallas_call | solution.py:215
  63.6 0.0 collective-permute-done.10.rest_2_
  63.6 0.0 collective-permute-done.3.rest_0_
  63.6 0.0 collective-permute-done.7.rest_1_
  63.6 2.4 %gram_tile.7 = f32[4,1024,1024]{2,1,0:T(8,128)} custom-call(f32[1]{0:T(128)S(6)} %copy.13.shrink_ref, bf16[256,1024]{1,0:T(8,128)(2,1)S(1)} %get-tuple-element.17.own_ref.rest_0_, bf16[256,1024]{1,0:T(8,128)(2,1)S(1)} %collective-permute-done.3.rest_0_, bf16[192,1024]{1,0:T(8,128)(2,1)S(1)} %collective-permute-done.7.rest_1_, ...), custom_call_target="tpu_custom_call", output_to_operand_aliasing={{}: (5, {})} | custom-call | flops 536870912 | bytes 5242880 | tf_op jit(solution)/shard_map/gram_tile/pallas_call | solution.py:215
  (3 shorter events, 0.0 us)
Async XLA Ops:
  2.5 6.7 %collective-permute-start = (bf16[64,1024]{1,0:T(8,128)(2,1)}, bf16[64,1024]{1,0:T(8,128)(2,1)S(1)}, u32[]{:S(2)}, u32[]{:S(2)}) collective-permute-start(bf16[64,1024]{1,0:T(8,128)(2,1)} %get-tuple-element.14), channel_id=1, source_target_pairs={{0,8},{8,0},{16,24},{24,16},{1,9},{9,1},{17,25},{25,17},{2,10},{10... | collective-permute-start | bytes 393224 | tf_op jit(solution)/shard_map/ppermute | solution.py:315
  5.5 5.2 %collective-permute-start.1 = (bf16[64,1024]{1,0:T(8,128)(2,1)}, bf16[64,1024]{1,0:T(8,128)(2,1)S(1)}, u32[]{:S(2)}, u32[]{:S(2)}) collective-permute-start(bf16[64,1024]{1,0:T(8,128)(2,1)} %get-tuple-element.15), channel_id=1, source_target_pairs={{0,16},{8,24},{16,0},{24,8},{1,17},{9,25},{17,1},{25,9},{2,18},{10... | collective-permute-start | bytes 393224 | tf_op jit(solution)/shard_map/ppermute | solution.py:315
  10.7 11.0 %collective-permute-start.5 = (bf16[128,1024]{1,0:T(8,128)(2,1)S(1)}, bf16[128,1024]{1,0:T(8,128)(2,1)S(1)}, u32[]{:S(2)}, u32[]{:S(2)}) collective-permute-start(bf16[128,1024]{1,0:T(8,128)(2,1)S(1)} %join.2), channel_id=1, source_target_pairs={{2,0},{3,1},{4,2},{5,3},{6,4},{7,5},{0,6},{1,7},{10,8},{11,9},{12,... | collective-permute-start | bytes 786440 | tf_op jit(solution)/shard_map/ppermute | solution.py:298
  14.4 7.3 %collective-permute-start.4 = (bf16[64,1024]{1,0:T(8,128)(2,1)}, bf16[64,1024]{1,0:T(8,128)(2,1)S(1)}, u32[]{:S(2)}, u32[]{:S(2)}) collective-permute-start(bf16[64,1024]{1,0:T(8,128)(2,1)} %get-tuple-element.12.block_ref), channel_id=1, source_target_pairs={{2,0},{3,1},{4,2},{5,3},{6,4},{7,5},{0,6},{1,7},{10,8},{11,9},{12,... | collective-permute-start | bytes 393224 | tf_op jit(solution)/shard_map/ppermute | solution.py:298
  14.8 11.2 %collective-permute-start.2 = (bf16[64,1024]{1,0:T(8,128)(2,1)}, bf16[64,1024]{1,0:T(8,128)(2,1)S(1)}, u32[]{:S(2)}, u32[]{:S(2)}) collective-permute-start(bf16[64,1024]{1,0:T(8,128)(2,1)} %get-tuple-element.16), channel_id=1, source_target_pairs={{0,24},{8,16},{16,8},{24,0},{1,25},{9,17},{17,9},{25,1},{2,26},{10... | collective-permute-start | bytes 393224 | tf_op jit(solution)/shard_map/ppermute | solution.py:315
  21.8 16.4 %collective-permute-start.6 = (bf16[192,1024]{1,0:T(8,128)(2,1)S(1)}, bf16[192,1024]{1,0:T(8,128)(2,1)S(1)}, u32[]{:S(2)}, u32[]{:S(2)}) collective-permute-start(bf16[192,1024]{1,0:T(8,128)(2,1)S(1)} %join.3), channel_id=1, source_target_pairs={{2,0},{3,1},{4,2},{5,3},{6,4},{7,5},{0,6},{1,7},{10,8},{11,9},{12,... | collective-permute-start | bytes 1179656 | tf_op jit(solution)/shard_map/ppermute | solution.py:298
  26.0 9.2 %collective-permute-start.8 = (bf16[64,1024]{1,0:T(8,128)(2,1)S(1)}, bf16[64,1024]{1,0:T(8,128)(2,1)S(1)}, u32[]{:S(2)}, u32[]{:S(2)}) collective-permute-start(bf16[64,1024]{1,0:T(8,128)(2,1)S(1)} %collective-permute-done.2.refs_3_), channel_id=1, source_target_pairs={{2,0},{3,1},{4,2},{5,3},{6,4},{7,5},{0,6},{1,7},{10,8},{11,9},{12,... | collective-permute-start | bytes 393224 | tf_op jit(solution)/shard_map/ppermute | solution.py:298
  26.7 0.9 %copy-start = (bf16[64,1024]{1,0:T(8,128)(2,1)S(1)}, bf16[64,1024]{1,0:T(8,128)(2,1)}, u32[]{:S(2)}) copy-start(bf16[64,1024]{1,0:T(8,128)(2,1)} %get-tuple-element.12.block_ref) | copy-start | bytes 393220
  27.6 0.7 %copy-start.1 = (s32[1024]{0:T(1024)S(1)}, s32[1024]{0:T(1024)}, u32[]{:S(2)}) copy-start(s32[1024]{0:T(1024)} %param.7) | copy-start | bytes 12292
  28.3 0.7 copy-start.2
  37.6 23.7 %collective-permute-start.11 = (bf16[256,1024]{1,0:T(8,128)(2,1)S(1)}, bf16[256,1024]{1,0:T(8,128)(2,1)S(1)}, u32[]{:S(2)}, u32[]{:S(2)}) collective-permute-start(bf16[256,1024]{1,0:T(8,128)(2,1)S(1)} %get-tuple-element.18), channel_id=1, source_target_pairs={{0,1},{1,0},{2,3},{3,2},{4,5},{5,4},{6,7},{7,6},{8,9},{9,8},{10,11... | collective-permute-start | bytes 1572872 | tf_op jit(solution)/shard_map/ppermute | solution.py:302
  37.6 26.0 %collective-permute-start.3 = (bf16[256,1024]{1,0:T(8,128)(2,1)S(1)}, bf16[256,1024]{1,0:T(8,128)(2,1)S(1)}, u32[]{:S(2)}, u32[]{:S(2)}) collective-permute-start(bf16[256,1024]{1,0:T(8,128)(2,1)S(1)} %get-tuple-element.17.own_ref.rest_0_), channel_id=1, source_target_pairs={{0,1},{1,0},{2,3},{3,2},{4,5},{5,4},{6,7},{7,6},{8,9},{9,8},{10,11... | collective-permute-start | bytes 1572872 | tf_op jit(solution)/shard_map/ppermute | solution.py:302
  38.1 25.5 %collective-permute-start.7 = (bf16[192,1024]{1,0:T(8,128)(2,1)S(1)}, bf16[192,1024]{1,0:T(8,128)(2,1)S(1)}, u32[]{:S(2)}, u32[]{:S(2)}) collective-permute-start(bf16[192,1024]{1,0:T(8,128)(2,1)S(1)} %collective-permute-done.6.rest_0_), channel_id=1, source_target_pairs={{0,1},{1,0},{2,3},{3,2},{4,5},{5,4},{6,7},{7,6},{8,9},{9,8},{10,11... | collective-permute-start | bytes 1179656 | tf_op jit(solution)/shard_map/ppermute | solution.py:302
  38.2 9.1 %collective-permute-start.9 = (bf16[64,1024]{1,0:T(8,128)(2,1)S(1)}, bf16[64,1024]{1,0:T(8,128)(2,1)S(1)}, u32[]{:S(2)}, u32[]{:S(2)}) collective-permute-start(bf16[64,1024]{1,0:T(8,128)(2,1)S(1)} %collective-permute-done.8.rest_2_), channel_id=1, source_target_pairs={{2,0},{3,1},{4,2},{5,3},{6,4},{7,5},{0,6},{1,7},{10,8},{11,9},{12,... | collective-permute-start | bytes 393224 | tf_op jit(solution)/shard_map/ppermute | solution.py:298
  42.5 1.2 %collective-permute-start.12 = (f32[8,128]{1,0:T(8,128)S(1)}, f32[8,128]{1,0:T(8,128)S(1)}, u32[]{:S(2)}, u32[]{:S(2)}) collective-permute-start(f32[8,128]{1,0:T(8,128)S(1)} %get-tuple-element.20), channel_id=1, source_target_pairs={{0,1},{1,0},{2,3},{3,2},{4,5},{5,4},{6,7},{7,6},{8,9},{9,8},{10,11... | collective-permute-start | bytes 12296 | tf_op jit(solution)/shard_map/ppermute | solution.py:302
  43.7 3.6 %collective-permute-start.13 = (f32[8,128]{1,0:T(8,128)S(1)}, f32[8,128]{1,0:T(8,128)S(1)}, u32[]{:S(2)}, u32[]{:S(2)}) collective-permute-start(f32[8,128]{1,0:T(8,128)S(1)} %add.3.rest_2_), channel_id=1, source_target_pairs={{2,0},{3,1},{4,2},{5,3},{6,4},{7,5},{0,6},{1,7},{10,8},{11,9},{12,... | collective-permute-start | bytes 12296 | tf_op jit(solution)/shard_map/ppermute | solution.py:298
  47.3 4.5 %collective-permute-start.14 = (f32[8,128]{1,0:T(8,128)S(1)}, f32[8,128]{1,0:T(8,128)S(1)}, u32[]{:S(2)}, u32[]{:S(2)}) collective-permute-start(f32[8,128]{1,0:T(8,128)S(1)} %add.3.rest_2_), channel_id=1, source_target_pairs={{4,0},{5,1},{6,2},{7,3},{0,4},{1,5},{2,6},{3,7},{12,8},{13,9},{14,... | collective-permute-start | bytes 12296 | tf_op jit(solution)/shard_map/ppermute | solution.py:298
  47.3 16.3 %collective-permute-start.10 = (bf16[64,1024]{1,0:T(8,128)(2,1)S(1)}, bf16[64,1024]{1,0:T(8,128)(2,1)S(1)}, u32[]{:S(2)}, u32[]{:S(2)}) collective-permute-start(bf16[64,1024]{1,0:T(8,128)(2,1)S(1)} %collective-permute-done.9.rest_1_), channel_id=1, source_target_pairs={{0,1},{1,0},{2,3},{3,2},{4,5},{5,4},{6,7},{7,6},{8,9},{9,8},{10,11... | collective-permute-start | bytes 393224 | tf_op jit(solution)/shard_map/ppermute | solution.py:302
  51.8 5.4 %collective-permute-start.15 = (f32[8,128]{1,0:T(8,128)S(1)}, f32[8,128]{1,0:T(8,128)S(1)}, u32[]{:S(2)}, u32[]{:S(2)}) collective-permute-start(f32[8,128]{1,0:T(8,128)S(1)} %add.3.rest_2_), channel_id=1, source_target_pairs={{6,0},{7,1},{0,2},{1,3},{2,4},{3,5},{4,6},{5,7},{14,8},{15,9},{8,1... | collective-permute-start | bytes 12296 | tf_op jit(solution)/shard_map/ppermute | solution.py:298
where the time goes:
time: 66.3 us; the launch traced here: 66 us
  waiting for transfers between devices  26.6 us (40%)
  starting transfers between devices  21.9 us (33%)
  Pallas kernels  13.9 us (21%)
  local copies, waits for them, and re-layouts  2.24 us (3%)
  between operations  1.41 us (2%)
    ppermute x8, waiting for transfers between devices, behind(): lax.ppermute(block, 'feat', [((i + 2 * k) % count, i) for i in range(coun...  22 us
    ppermute x8, starting transfers between devices, behind(): lax.ppermute(block, 'feat', [((i + 2 * k) % count, i) for i in range(coun...  15.1 us
    pallas_call x4, Pallas kernels, tile(): pl.pallas_call(body, out_shape=out_shape, in_specs=in_specs, out_specs=ou...  9.48 us
    ppermute x3, starting transfers between devices, shards(): blocks.append(lax.ppermute(sent[k], 'layer', route))  6.04 us
    ppermute x3, waiting for transfers between devices, shards(): blocks.append(lax.ppermute(sent[k], 'layer', route))  3.66 us
    unnamed x6, local copies, waits for them, and re-layouts  2.24 us
    pallas_call x1, Pallas kernels, select(): pl.pallas_call(body, out_shape=[jax.ShapeDtypeStruct((rows, width), acts....  1.87 us
    pallas_call x1, Pallas kernels, far_tile(): pl.pallas_call(body, out_shape=jax.ShapeDtypeStruct((rows, width), jnp.fl...  1.67 us
  transfers between devices with their start and end apart: 16, of which 8 were waited for; matrix products, arithmetic and copies ran while one was open for 0% of the time, Pallas kernels for 14%

commit v1 on v0

v1 whole, which is shorter than its diff:
```python
import math

import jax
import jax.numpy as jnp
from jax import lax
from jax.experimental import pallas as pl
from jax.experimental.pallas import tpu as pltpu
from jax.sharding import PartitionSpec as P

TRANSPOSED = (((0,), (0,)), ((), ()))
SMEM = pl.BlockSpec(memory_space=pltpu.SMEM)
VMEM = pl.BlockSpec(memory_space=pltpu.VMEM)
HBM = pl.BlockSpec(memory_space=pltpu.HBM)
ANY = pl.BlockSpec(memory_space=pl.ANY)


def room(*shapes):
    total = sum(math.prod(shape) * jnp.dtype(dtype).itemsize for shape, dtype in shapes)
    return pltpu.CompilerParams(vmem_limit_bytes=total + (2 << 20))


def like(*arrays):
    return [(a.shape, a.dtype) for a in arrays]


def partner(i, k, count):
    return (i + k) % count if count & (count - 1) else i ^ k


def select(acts, layer_order):
    layers, rows, width = acts.shape

    def body(order_ref, acts_ref, *rest):
        outs, (held, order, sem) = rest[:layers], rest[layers:]
        copies = [
            pltpu.make_async_copy(order_ref, order, sem.at[0]),
            pltpu.make_async_copy(acts_ref, held, sem.at[1]),
        ]
        for copy in copies:
            copy.start()
        here = lax.axis_index("layer")
        copies[0].wait()
        slots = []
        for k in range(layers):
            layer = partner(here, k, layers)
            slot = jnp.int32(0)
            for s in range(1, layers):
                slot = jnp.where(order[0, s] == layer, s, slot)
            slots.append(slot)
        copies[1].wait()
        outs[0][:rows, :] = held[slots[0]]
        outs[0][rows:, :] = held[slots[1]]
        for out, slot in zip(outs[1:], slots[1:]):
            out[...] = held[slot]

    return pl.pallas_call(
        body,
        out_shape=[jax.ShapeDtypeStruct((2 * rows, width), acts.dtype)]
        + [jax.ShapeDtypeStruct((rows, width), acts.dtype)] * (layers - 1),
        in_specs=[ANY, ANY],
        out_specs=[VMEM] * layers,
        scratch_shapes=[
            pltpu.VMEM(acts.shape, acts.dtype),
            pltpu.SMEM(layer_order.shape, layer_order.dtype),
            pltpu.SemaphoreType.DMA((2,)),
        ],
        name="select",
    )(layer_order, acts)


def prepare(block, rows, groups, group_scale):
    count = group_scale.shape[1]
    line = (1, groups.shape[0])

    def body(scale_hbm, groups_hbm, block_hbm, out_ref, gains_ref, scale, held, sem):
        copies = [
            pltpu.make_async_copy(scale_hbm, scale, sem.at[0]),
            pltpu.make_async_copy(groups_hbm, held, sem.at[1]),
            pltpu.make_async_copy(block_hbm.at[pl.ds(0, rows), :], out_ref, sem.at[2]),
        ]
        for copy in copies:
            copy.start()
        for copy in copies:
            copy.wait()
        value = jnp.zeros(line, jnp.float32)
        for g in range(count):
            value = jnp.where(held[...] == g, scale[0, g], value)
        gains_ref[...] = value

    return pl.pallas_call(
        body,
        out_shape=[
            jax.ShapeDtypeStruct((rows, block.shape[1]), block.dtype),
            jax.ShapeDtypeStruct(line, jnp.float32),
        ],
        in_specs=[ANY] * 3,
        out_specs=[VMEM] * 2,
        scratch_shapes=[
            pltpu.SMEM(group_scale.shape, group_scale.dtype),
            pltpu.VMEM(line, groups.dtype),
            pltpu.SemaphoreType.DMA((3,)),
        ],
        compiler_params=room(*like(block, block, groups, groups)),
        name="prepare",
    )(group_scale, groups[None], block)


def join(*pieces):
    if len(pieces) == 1 and pieces[0][2] == pieces[0][0].shape[0]:
        return pieces[0][0]
    total = sum(rows for _, _, rows in pieces)
    arrays = [piece[0] for piece in pieces]
    width, dtype = arrays[0].shape[1], arrays[0].dtype

    def body(*refs):
        at = 0
        for ref, (_, start, rows) in zip(refs, pieces):
            refs[-1][at : at + rows, :] = ref[start : start + rows, :]
            at += rows

    return pl.pallas_call(
        body,
        out_shape=jax.ShapeDtypeStruct((total, width), dtype),
        in_specs=[VMEM] * len(arrays),
        out_specs=VMEM,
        compiler_params=room(*like(*arrays), ((total, width), dtype)),
        name="join",
    )(*arrays)


def chip_trace(own, other):
    tokens = own.shape[0]

    def body(own_ref, other_ref, out_ref):
        total = jnp.zeros((1, own.shape[1]), jnp.float32)
        for ref in (own_ref, other_ref):
            value = ref[...].astype(jnp.float32)
            total = total + jnp.sum(value * value, axis=0, keepdims=True)
        out_ref[...] = jnp.broadcast_to(jnp.sum(total) / tokens, out_ref.shape)

    return pl.pallas_call(
        body,
        out_shape=jax.ShapeDtypeStruct((8, 128), jnp.float32),
        in_specs=[VMEM] * 2,
        out_specs=VMEM,
        compiler_params=room(*like(own, other)),
        name="chip_trace",
    )(own, other)


def place():
    f = lax.axis_index("feat")
    return f, f // 2, f % 2


def assemble(panel_ref, blocks):
    start = 0
    for block in blocks:
        panel_ref[start : start + block.shape[0], :] = block[...]
        start += block.shape[0]


def fill(stack, count, own, tasks, shrink, keep=False, patch=()):
    tokens, width = own.shape
    given = [block for even, odd, _ in tasks for block in (*even, *odd)]
    step = next(s for s in (128, 64, 32, 16, 8, width) if width % s == 0)
    steps = width // step
    lines = [slice(i * step, (i + 1) * step) for i in range(steps)]

    def body(shrink_ref, own_ref, *rest):
        parts, rest = rest[: len(given)], rest[len(given) :]
        added, rest = rest[: len(patch)], rest[len(patch) :]
        rest = rest[(stack is not None) :]
        out_ref, rest = rest[0], rest[1:]
        if keep:
            corner_ref, rest = rest[0], rest[1:]
        panel, buffer, fixed, sem = rest
        _, _, core = place()
        scale = (1.0 - shrink_ref[0]) * (1.0 / tokens)
        copies = []

        def write(source, target):
            copies.append(pltpu.make_async_copy(source, target, sem.at[len(copies)]))
            copies[-1].start()

        for t, (even, odd, index) in enumerate(tasks):
            first, parts = parts[: len(even)], parts[len(even) :]
            second, parts = parts[: len(odd)], parts[len(odd) :]
            if odd:
                pl.when(core == 0)(lambda first=first: assemble(panel, first))
                pl.when(core != 0)(lambda second=second: assemble(panel, second))
            else:
                assemble(panel, first)
            to = index(core)
            for rows in lines:
                value = lax.dot_general(
                    own_ref[:, rows],
                    panel[...],
                    TRANSPOSED,
                    preferred_element_type=jnp.float32,
                )
                value = value * scale
                buffer[t, rows, :] = value
                if keep and t == len(tasks) - 1:
                    corner_ref[rows, :] = value[:, rows]
                write(buffer.at[t, rows, :], out_ref.at[to, rows, :])
        if patch:
            corner, gains_ref, sums = added[0], added[1], added[2:]
            trace = sums[0][0:1, 0:1]
            for other in sums[1:]:
                trace = trace + other[0:1, 0:1]
            mu = trace * (1.0 / (width * lax.axis_size("feat")))
            line = gains_ref[...] * (mu * shrink_ref[0])
            same = lax.broadcasted_iota(jnp.int32, (step, step), 0) == lax.broadcasted_iota(
                jnp.int32, (step, step), 1
            )
            for rows in lines:
                fixed[rows, :] = corner[rows, :] + jnp.where(same, line[:, rows], 0.0)
                write(fixed.at[rows, :], out_ref.at[0, rows, rows])
        for copy in copies:
            copy.wait()

    out_shape = [jax.ShapeDtypeStruct((count, width, width), jnp.float32)]
    out_specs = [ANY]
    if keep:
        out_shape.append(jax.ShapeDtypeStruct((width, step), jnp.float32))
        out_specs.append(VMEM)
    held = ((len(tasks) + 1, width, width), jnp.float32)
    operands = [shrink, own, *given, *patch] + ([] if stack is None else [stack])
    in_specs = [SMEM] + [VMEM] * (1 + len(given) + len(patch)) + [ANY] * (stack is not None)
    outs = pl.pallas_call(
        body,
        out_shape=out_shape,
        in_specs=in_specs,
        out_specs=out_specs,
        scratch_shapes=[
            pltpu.VMEM((tokens, width), own.dtype),
            pltpu.VMEM((len(tasks), width, width), jnp.float32),
            pltpu.VMEM((width, step), jnp.float32),
            pltpu.SemaphoreType.DMA((steps * (len(tasks) + 1),)),
        ],
        input_output_aliases={} if stack is None else {len(operands) - 1: 0},
        compiler_params=room(*like(own, own, *given, *patch), held),
        cost_estimate=pl.CostEstimate(
            flops=2 * tokens * width * width * len(tasks),
            bytes_accessed=(4 * width * width + 4 * tokens * width) * len(tasks),
            transcendentals=0,
        ),
        name="gram_tiles",
    )(*operands)
    return outs if keep else outs[0]


def far_tile(own, blocks, shrink):
    tokens, width = own.shape
    rows = width // 2

    step = next(s for s in (128, 64, 32, 16, 8, rows) if rows % s == 0)
    steps = rows // step

    def body(shrink_ref, own_ref, *rest):
        parts, (out_ref, left, panel, buffer, sem) = rest[: len(blocks)], rest[len(blocks) :]
        f, _, _ = place()
        lower = f < lax.axis_size("feat") // 2
        scale = (1.0 - shrink_ref[0]) * (1.0 / tokens)
        assemble(panel, parts)

        @pl.when(lower)
        def _():
            left[...] = own_ref[:, :rows]

        @pl.when(jnp.logical_not(lower))
        def _():
            left[...] = panel[:, rows:]
            panel[...] = own_ref[...]

        copies = []
        for i in range(steps):
            part = slice(i * step, (i + 1) * step)
            buffer[part, :] = (
                lax.dot_general(
                    left[:, part],
                    panel[...],
                    TRANSPOSED,
                    preferred_element_type=jnp.float32,
                )
                * scale
            )
            copies.append(
                pltpu.make_async_copy(buffer.at[part, :], out_ref.at[part, :], sem.at[i])
            )
            copies[-1].start()
        for copy in copies:
            copy.wait()

    return pl.pallas_call(
        body,
        out_shape=jax.ShapeDtypeStruct((rows, width), jnp.float32),
        in_specs=[SMEM] + [VMEM] * (1 + len(blocks)),
        out_specs=ANY,
        scratch_shapes=[
            pltpu.VMEM((tokens, rows), own.dtype),
            pltpu.VMEM((tokens, width), own.dtype),
            pltpu.VMEM((rows, width), jnp.float32),
            pltpu.SemaphoreType.DMA((steps,)),
        ],
        compiler_params=room(*like(own, own, own, *blocks), ((width, width), jnp.float32)),
        cost_estimate=pl.CostEstimate(
            flops=2 * tokens * rows * width,
            bytes_accessed=4 * rows * width + 4 * tokens * width,
            transcendentals=0,
        ),
        name="far_tile",
    )(shrink, own, *blocks)


def behind(block, k):
    count = lax.axis_size("feat")
    return lax.ppermute(block, "feat", [((i + 2 * k) % count, i) for i in range(count)])


def paired(block, k):
    chips = lax.axis_size("feat") // 2
    pairs = [(z, partner(z, k, chips)) for z in range(chips)]
    return lax.ppermute(block, "feat", [(2 * s + c, 2 * d + c) for s, d in pairs for c in (0, 1)])


def swapped(block):
    return lax.ppermute(block, "feat", [(i, i ^ 1) for i in range(lax.axis_size("feat"))])


def shards(acts, layer_order, groups, group_scale, shrink):
    layers, _, _ = acts.shape
    half = lax.axis_size("feat") // 2
    chips = half
    reach = chips // 2

    pair, *sent = select(acts, layer_order)
    rows = acts.shape[1]

    def exchanged(block, k):
        route = [(i, partner(i, k, layers)) for i in range(layers)]
        return lax.ppermute(block, "layer", route)

    def onward(block):
        return behind(block, 1)

    got = [exchanged(block, k + 1) for k, block in enumerate(sent)]
    first, gains = prepare(pair, rows, groups, group_scale)

    near = onward(pair)
    middle = join(*[(block, 0, rows) for block in got[1:-1]])
    middle_near = onward(middle)
    last_near = onward(got[-1])
    crossed = exchanged(join((near, rows, rows)), 1)
    parts = [
        join((near, 0, rows), (middle_near, 0, middle.shape[0])),
        join((crossed, 0, rows), (last_near, 0, rows)),
    ]
    ahead = [None, parts]
    for _ in range(2, reach + 1):
        parts = [onward(block) for block in parts]
        ahead.append(parts)

    own = join(*[(block, 0, block.shape[0]) for block in (first, middle, got[0], got[-1])])
    beside = swapped(own)
    stack, corner = fill(None, half, own, [([own], (), lambda core: 0)], shrink, keep=True)
    part = chip_trace(own, beside)
    sums = [part]
    for k in range(1, chips):
        sums.append(paired(part, k))
    tasks = []
    for k in range(1, reach):
        other = []
        for block in ahead[k]:
            other.append(swapped(block))
        tasks.append((ahead[k], (), lambda core, k=k: 2 * k))
        tasks.append((other, (), lambda core, k=k: jnp.where(core == 0, 2 * k + 1, 2 * k - 1)))
    for t in range(0, len(tasks), 2):
        stack = fill(stack, half, own, tasks[t : t + 2], shrink)
    odd = []
    for block in ahead[reach]:
        odd.append(swapped(block))
    far = far_tile(own, ahead[reach], shrink)
    index = lambda core: jnp.where(core == 0, 1, half - 1)
    patch = [corner, gains, *sums]
    stack = fill(stack, half, own, [([beside], odd, index)], shrink, patch=patch)
    return (stack[None, None], far[None, None])


def solution(mesh):
    placed = (P(None, "layer", "feat"), P("layer", None), P("feat"), P("layer", None), P("layer"))

    return jax.shard_map(
        shards,
        mesh=mesh,
        in_specs=placed,
        out_specs=(P("layer", "feat", None, None, None), P("layer", "feat", None, None)),
        check_vma=False,
    )
```

time: 66.3 us -> 52 us (0.78)
  waiting for transfers between devices: 26.6 us -> 15.7 us
  starting transfers between devices: 21.9 us -> 19.1 us
    ppermute x8 -> x5, waiting for transfers between devices: 22 us -> 10.8 us  [behind(): lax.ppermute(block, 'feat', [((i + 2 * k) % count, i) for i in range(coun...]
    ppermute x8 -> x5, starting transfers between devices: 15.1 us -> 9.04 us  [behind(): lax.ppermute(block, 'feat', [((i + 2 * k) % count, i) for i in range(coun...]
    ppermute x3 -> x7, starting transfers between devices: 6.04 us -> 9.5 us  [the longest x4 5.04 us: exchanged(): return lax.ppermute(block, 'layer', route)]
    ppermute x3 -> x7, waiting for transfers between devices: 3.66 us -> 4.83 us  [the longest x4 4.82 us: exchanged(): return lax.ppermute(block, 'layer', route)]
    ppermute x5, waiting for transfers between devices: 1.03 us -> 0.01 us  [swapped(): lax.ppermute(block, 'feat', [(i, i ^ 1) for i in range(lax.axis_size('fea...]
    pallas_call x9 -> x10, Pallas kernels: 12.2 us -> 11.6 us  [the longest x3 8.79 us: fill(): pl.pallas_call(body, out_shape=out_shape, in_specs=in_specs, out_specs=ou...]
  transfers between devices with their start and end apart: 16 -> 17, of which waited for: 8 -> 4; matrix products, arithmetic and copies ran while one was open for 0% -> 0% of each run, Pallas kernels for 14% -> 17%
where the time goes in v1:
time: 52 us; the launch traced here: 51.8 us
  starting transfers between devices  19.1 us (37%)
  waiting for transfers between devices  15.7 us (30%)
  Pallas kernels  13.3 us (26%)
  local copies, waits for them, and re-layouts  2.29 us (4%)
  between operations  1.44 us (3%)
    ppermute x5, waiting for transfers between devices, behind(): lax.ppermute(block, 'feat', [((i + 2 * k) % count, i) for i in range(coun...  10.8 us
    ppermute x5, starting transfers between devices, behind(): lax.ppermute(block, 'feat', [((i + 2 * k) % count, i) for i in range(coun...  9.04 us
    pallas_call x3, Pallas kernels, fill(): pl.pallas_call(body, out_shape=out_shape, in_specs=in_specs, out_specs=ou...  8.79 us
    ppermute x4, starting transfers between devices, exchanged(): return lax.ppermute(block, 'layer', route)  5.04 us
    ppermute x4, waiting for transfers between devices, exchanged(): return lax.ppermute(block, 'layer', route)  4.82 us
    ppermute x3, starting transfers between devices, paired(): lax.ppermute(block, 'feat', [(2 * s + c, 2 * d + c) for s, d in pairs for...  4.45 us
    unnamed x6, local copies, waits for them, and re-layouts  2.29 us
    pallas_call x1, Pallas kernels, select(): pl.pallas_call(body, out_shape=[jax.ShapeDtypeStruct((2 * rows, width), a...  1.92 us
  transfers between devices with their start and end apart: 17, of which 4 were waited for; matrix products, arithmetic and copies ran while one was open for 0% of the time, Pallas kernels for 17%

profile of v1, /device:TPU:0, one launch (start us, length us, event | category | flops | bytes accessed | tf_op | source)
XLA Modules:
  0.0 51.8 jit_solution(3739862037098469496)
XLA Ops:
  0.6 1.9 %select.1 = (bf16[128,1024]{1,0:T(8,128)(2,1)}, bf16[64,1024]{1,0:T(8,128)(2,1)}, bf16[64,1024]{1,0:T(8,128)(2,1)}, bf16[64,1024]{1,0:T(8,128)(2,1)}) custom-call(s32[1,4]{1,0:T(1,128)} %order_ref.1, bf16[4,64,1024]{2,1,0:T(8,128)(2,1)} %acts_ref.1), custom_call_target="tpu_custom_call" | custom-call | tf_op jit(solution)/shard_map/select/pallas_call | solution.py:56
  2.6 5.1 %collective-permute-start.4 = (bf16[128,1024]{1,0:T(8,128)(2,1)}, bf16[128,1024]{1,0:T(8,128)(2,1)S(1)}, u32[]{:S(2)}, u32[]{:S(2)}) collective-permute-start(bf16[128,1024]{1,0:T(8,128)(2,1)} %get-tuple-element.10.block_hbm), channel_id=1, source_target_pairs={{2,0},{3,1},{4,2},{5,3},{6,4},{7,5},{0,6},{1,7},{10,8},{11,9},{12,... | collective-permute-start | bytes 786440 | tf_op jit(solution)/shard_map/ppermute | solution.py:319
  7.7 1.5 %collective-permute-start = (bf16[64,1024]{1,0:T(8,128)(2,1)}, bf16[64,1024]{1,0:T(8,128)(2,1)S(1)}, u32[]{:S(2)}, u32[]{:S(2)}) collective-permute-start(bf16[64,1024]{1,0:T(8,128)(2,1)} %get-tuple-element.12), channel_id=1, source_target_pairs={{0,16},{8,24},{16,0},{24,8},{1,17},{9,25},{17,1},{25,9},{2,18},{10... | collective-permute-start | bytes 393224 | tf_op jit(solution)/shard_map/ppermute | solution.py:343
  9.2 1.4 %collective-permute-start.2 = (bf16[64,1024]{1,0:T(8,128)(2,1)}, bf16[64,1024]{1,0:T(8,128)(2,1)S(1)}, u32[]{:S(2)}, u32[]{:S(2)}) collective-permute-start(bf16[64,1024]{1,0:T(8,128)(2,1)} %get-tuple-element.14), channel_id=1, source_target_pairs={{0,24},{8,16},{16,8},{24,0},{1,25},{9,17},{17,9},{25,1},{2,26},{10... | collective-permute-start | bytes 393224 | tf_op jit(solution)/shard_map/ppermute | solution.py:343
  10.6 0.5 %collective-permute-start.1 = (bf16[64,1024]{1,0:T(8,128)(2,1)}, bf16[64,1024]{1,0:T(8,128)(2,1)S(1)}, u32[]{:S(2)}, u32[]{:S(2)}) collective-permute-start(bf16[64,1024]{1,0:T(8,128)(2,1)} %get-tuple-element.13), channel_id=1, source_target_pairs={{0,8},{8,0},{16,24},{24,16},{1,9},{9,1},{17,25},{25,17},{2,10},{10... | collective-permute-start | bytes 393224 | tf_op jit(solution)/shard_map/ppermute | solution.py:343
  11.2 3.7 %collective-permute-done.refs_1_ = bf16[64,1024]{1,0:T(8,128)(2,1)S(1)} collective-permute-done((bf16[64,1024]{1,0:T(8,128)(2,1)}, bf16[64,1024]{1,0:T(8,128)(2,1)S(1)}, u32[]{:S(2)}, u32[]{:S(2)}) %collective-permute-start) | collective-permute-done | bytes 131104 | tf_op jit(solution)/shard_map/ppermute | solution.py:343
  14.8 0.4 collective-permute-start.5
  15.3 1.2 %collective-permute-done.2.refs_3_ = bf16[64,1024]{1,0:T(8,128)(2,1)S(1)} collective-permute-done((bf16[64,1024]{1,0:T(8,128)(2,1)}, bf16[64,1024]{1,0:T(8,128)(2,1)S(1)}, u32[]{:S(2)}, u32[]{:S(2)}) %collective-permute-start.2) | collective-permute-done | bytes 131104 | tf_op jit(solution)/shard_map/ppermute | solution.py:343
  16.4 0.4 collective-permute-start.9
  16.9 0.0 collective-permute-done.4.refs_0_
  16.9 1.6 %collective-permute-start.8 = (bf16[64,1024]{1,0:T(8,128)(2,1)S(1)}, bf16[64,1024]{1,0:T(8,128)(2,1)S(1)}, u32[]{:S(2)}, u32[]{:S(2)}) collective-permute-start(bf16[64,1024]{1,0:T(8,128)(2,1)S(1)} %join.6), channel_id=1, source_target_pairs={{0,8},{8,0},{16,24},{24,16},{1,9},{9,1},{17,25},{25,17},{2,10},{10... | collective-permute-start | bytes 393224 | tf_op jit(solution)/shard_map/ppermute | solution.py:343
  18.5 0.0 copy-start
  18.5 0.9 %copy-done = bf16[128,1024]{1,0:T(8,128)(2,1)S(1)} copy-done((bf16[128,1024]{1,0:T(8,128)(2,1)S(1)}, bf16[128,1024]{1,0:T(8,128)(2,1)}, u32[]{:S(2)}) %copy-start) | copy-done | bytes 262168
  19.4 0.0 copy-start.1
  19.4 0.7 %copy-done.1 = s32[1024]{0:T(1024)S(1)} copy-done((s32[1024]{0:T(1024)S(1)}, s32[1024]{0:T(1024)}, u32[]{:S(2)}) %copy-start.1) | copy-done | bytes 4120
  20.1 0.0 copy-start.2
  20.1 0.7 %copy-done.2 = f32[1,64]{1,0:T(1,128)S(1)} copy-done((f32[1,64]{1,0:T(1,128)S(1)}, f32[1,64]{1,0:T(1,128)}, u32[]{:S(2)}) %copy-start.2) | copy-done | bytes 280
  20.8 0.6 %prepare.1 = (bf16[64,1024]{1,0:T(8,128)(2,1)S(1)}, f32[1,1024]{1,0:T(1,128)S(1)}) custom-call(f32[1,64]{1,0:T(1,128)S(1)} %copy-done.2, s32[1,1024]{1,0:T(1,128)S(1)} %bitcast.3, bf16[128,1024]{1,0:T(8,128)(2,1)S(1)} %copy-done), custom_call_target="tpu_custom_call" | custom-call | tf_op jit(solution)/shard_map/prepare/pallas_call | solution.py:90
  21.4 0.0 collective-permute-done.1.refs_2_
  21.4 0.1 collective-permute-start.3
  21.5 0.0 collective-permute-done.5.refs_1_
  21.5 2.0 %collective-permute-start.6 = (bf16[128,1024]{1,0:T(8,128)(2,1)S(1)}, bf16[128,1024]{1,0:T(8,128)(2,1)S(1)}, u32[]{:S(2)}, u32[]{:S(2)}) collective-permute-start(bf16[128,1024]{1,0:T(8,128)(2,1)S(1)} %join.5.rest_0_), channel_id=1, source_target_pairs={{2,0},{3,1},{4,2},{5,3},{6,4},{7,5},{0,6},{1,7},{10,8},{11,9},{12,... | collective-permute-start | bytes 786440 | tf_op jit(solution)/shard_map/ppermute | solution.py:319
  23.6 0.0 collective-permute-done.9.refs_1_
  23.6 0.0 collective-permute-done.8.refs_0_
  23.6 1.0 %collective-permute-start.10 = (bf16[128,1024]{1,0:T(8,128)(2,1)S(1)}, bf16[128,1024]{1,0:T(8,128)(2,1)S(1)}, u32[]{:S(2)}, u32[]{:S(2)}) collective-permute-start(bf16[128,1024]{1,0:T(8,128)(2,1)S(1)} %join.7.rest_1_), channel_id=1, source_target_pairs={{2,0},{3,1},{4,2},{5,3},{6,4},{7,5},{0,6},{1,7},{10,8},{11,9},{12,... | collective-permute-start | bytes 786440 | tf_op jit(solution)/shard_map/ppermute | solution.py:319
  24.6 0.0 collective-permute-start.15
  24.6 0.5 collective-permute-start.16
  25.1 5.7 %collective-permute-done.6.rest_0_ = bf16[128,1024]{1,0:T(8,128)(2,1)S(1)} collective-permute-done((bf16[128,1024]{1,0:T(8,128)(2,1)S(1)}, bf16[128,1024]{1,0:T(8,128)(2,1)S(1)}, u32[]{:S(2)}, u32[]{:S(2)}) %collective-permute-start.6) | collective-permute-done | bytes 262176 | tf_op jit(solution)/shard_map/ppermute | solution.py:319
  30.8 0.0 collective-permute-start.7
  30.8 5.1 %collective-permute-done.10.rest_1_ = bf16[128,1024]{1,0:T(8,128)(2,1)S(1)} collective-permute-done((bf16[128,1024]{1,0:T(8,128)(2,1)S(1)}, bf16[128,1024]{1,0:T(8,128)(2,1)S(1)}, u32[]{:S(2)}, u32[]{:S(2)}) %collective-permute-start.10) | collective-permute-done | bytes 262176 | tf_op jit(solution)/shard_map/ppermute | solution.py:319
  35.9 0.0 collective-permute-start.11
  36.6 2.4 %gram_tiles.3 = (f32[4,1024,1024]{2,1,0:T(8,128)}, f32[1024,128]{1,0:T(8,128)S(1)}) custom-call(f32[1]{0:T(128)S(6)} %copy.11.shrink_ref, bf16[256,1024]{1,0:T(8,128)(2,1)S(1)} %join.4.own_ref.rest_0_, bf16[256,1024]{1,0:T(8,128)(2,1)S(1)} %join.4.own_ref.rest_0_), custom_call_target="tpu_custom_call" | custom-call | flops 536870912 | bytes 5242880 | tf_op jit(solution)/shard_map/gram_tiles/pallas_call | solution.py:231
  39.0 0.0 collective-permute-done.3.other_ref.rest_0_
  39.0 0.2 chip_trace.1.rest_5_
  39.2 1.6 %collective-permute-start.12 = (f32[8,128]{1,0:T(8,128)S(1)}, f32[8,128]{1,0:T(8,128)S(1)}, u32[]{:S(2)}, u32[]{:S(2)}) collective-permute-start(f32[8,128]{1,0:T(8,128)S(1)} %chip_trace.1.rest_5_), channel_id=1, source_target_pairs={{0,2},{1,3},{2,0},{3,1},{4,6},{5,7},{6,4},{7,5},{8,10},{9,11},{10,... | collective-permute-start | bytes 12296 | tf_op jit(solution)/shard_map/ppermute | solution.py:325
  40.8 0.0 collective-permute-done.15.rest_2_
  40.8 2.8 %collective-permute-start.13 = (f32[8,128]{1,0:T(8,128)S(1)}, f32[8,128]{1,0:T(8,128)S(1)}, u32[]{:S(2)}, u32[]{:S(2)}) collective-permute-start(f32[8,128]{1,0:T(8,128)S(1)} %chip_trace.1.rest_5_), channel_id=1, source_target_pairs={{0,4},{1,5},{2,6},{3,7},{4,0},{5,1},{6,2},{7,3},{8,12},{9,13},{10,... | collective-permute-start | bytes 12296 | tf_op jit(solution)/shard_map/ppermute | solution.py:325
  43.6 0.0 collective-permute-done.16.rest_3_
  43.6 0.1 collective-permute-start.14
  43.6 3.8 %gram_tiles.4.rest_9_ = f32[4,1024,1024]{2,1,0:T(8,128)} custom-call(f32[1]{0:T(128)S(6)} %copy.11.shrink_ref, bf16[256,1024]{1,0:T(8,128)(2,1)S(1)} %join.4.own_ref.rest_0_, bf16[128,1024]{1,0:T(8,128)(2,1)S(1)} %join.5.rest_0_, bf16[128,1024]{1,0:T(8,128)(2,1)S(1)} %join.7.rest_1_, ...), custom_call_target="tpu_custom_call", output_to_operand_aliasing={{}: (6, {})} | custom-call | flops 1073741824 | bytes 10485760 | tf_op jit(solution)/shard_map/gram_tiles/pallas_call | solution.py:231
  47.4 1.7 %far_tile.1 = f32[512,1024]{1,0:T(8,128)} custom-call(f32[1]{0:T(128)S(6)} %copy.11.shrink_ref, bf16[256,1024]{1,0:T(8,128)(2,1)S(1)} %join.4.own_ref.rest_0_, bf16[128,1024]{1,0:T(8,128)(2,1)S(1)} %collective-permute-done.6.rest_0_, bf16[128,1024]{1,0:T(8,128)(2,1)S(1)} %collective-permute-done.10.rest_1_), custom_call_target="tpu_custom_call" | custom-call | flops 268435456 | bytes 3145728 | tf_op jit(solution)/shard_map/far_tile/pallas_call | solution.py:296
  49.1 0.0 collective-permute-done.12.rest_6_
  49.1 0.0 collective-permute-done.13.rest_7_
  49.1 0.0 collective-permute-done.14.rest_8_
  49.1 0.0 collective-permute-done.7.rest_1_
  49.1 0.0 collective-permute-done.11.rest_2_
  49.1 2.6 %gram_tiles.5 = f32[4,1024,1024]{2,1,0:T(8,128)} custom-call(f32[1]{0:T(128)S(6)} %copy.11.shrink_ref, bf16[256,1024]{1,0:T(8,128)(2,1)S(1)} %join.4.own_ref.rest_0_, bf16[256,1024]{1,0:T(8,128)(2,1)S(1)} %collective-permute-done.3.other_ref.rest_0_, bf16[128,1024]{1,0:T(8,128)(2,1)S(1)} %collective-permute-done.7.rest_1_, ...), custom_call_target="tpu_custom_call", output_to_operand_aliasing={{}: (11, {})} | custom-call | flops 536870912 | bytes 5242880 | tf_op jit(solution)/shard_map/gram_tiles/pallas_call | solution.py:231
  (4 shorter events, 0.1 us)
Async XLA Ops:
  2.6 14.3 %collective-permute-start.4 = (bf16[128,1024]{1,0:T(8,128)(2,1)}, bf16[128,1024]{1,0:T(8,128)(2,1)S(1)}, u32[]{:S(2)}, u32[]{:S(2)}) collective-permute-start(bf16[128,1024]{1,0:T(8,128)(2,1)} %get-tuple-element.10.block_hbm), channel_id=1, source_target_pairs={{2,0},{3,1},{4,2},{5,3},{6,4},{7,5},{0,6},{1,7},{10,8},{11,9},{12,... | collective-permute-start | bytes 786440 | tf_op jit(solution)/shard_map/ppermute | solution.py:319
  7.7 7.2 %collective-permute-start = (bf16[64,1024]{1,0:T(8,128)(2,1)}, bf16[64,1024]{1,0:T(8,128)(2,1)S(1)}, u32[]{:S(2)}, u32[]{:S(2)}) collective-permute-start(bf16[64,1024]{1,0:T(8,128)(2,1)} %get-tuple-element.12), channel_id=1, source_target_pairs={{0,16},{8,24},{16,0},{24,8},{1,17},{9,25},{17,1},{25,9},{2,18},{10... | collective-permute-start | bytes 393224 | tf_op jit(solution)/shard_map/ppermute | solution.py:343
  9.2 7.2 %collective-permute-start.2 = (bf16[64,1024]{1,0:T(8,128)(2,1)}, bf16[64,1024]{1,0:T(8,128)(2,1)S(1)}, u32[]{:S(2)}, u32[]{:S(2)}) collective-permute-start(bf16[64,1024]{1,0:T(8,128)(2,1)} %get-tuple-element.14), channel_id=1, source_target_pairs={{0,24},{8,16},{16,8},{24,0},{1,25},{9,17},{17,9},{25,1},{2,26},{10... | collective-permute-start | bytes 393224 | tf_op jit(solution)/shard_map/ppermute | solution.py:343
  10.6 10.7 %collective-permute-start.1 = (bf16[64,1024]{1,0:T(8,128)(2,1)}, bf16[64,1024]{1,0:T(8,128)(2,1)S(1)}, u32[]{:S(2)}, u32[]{:S(2)}) collective-permute-start(bf16[64,1024]{1,0:T(8,128)(2,1)} %get-tuple-element.13), channel_id=1, source_target_pairs={{0,8},{8,0},{16,24},{24,16},{1,9},{9,1},{17,25},{25,17},{2,10},{10... | collective-permute-start | bytes 393224 | tf_op jit(solution)/shard_map/ppermute | solution.py:343
  14.8 6.7 %collective-permute-start.5 = (bf16[64,1024]{1,0:T(8,128)(2,1)S(1)}, bf16[64,1024]{1,0:T(8,128)(2,1)S(1)}, u32[]{:S(2)}, u32[]{:S(2)}) collective-permute-start(bf16[64,1024]{1,0:T(8,128)(2,1)S(1)} %collective-permute-done.refs_1_), channel_id=1, source_target_pairs={{2,0},{3,1},{4,2},{5,3},{6,4},{7,5},{0,6},{1,7},{10,8},{11,9},{12,... | collective-permute-start | bytes 393224 | tf_op jit(solution)/shard_map/ppermute | solution.py:319
  16.4 7.1 %collective-permute-start.9 = (bf16[64,1024]{1,0:T(8,128)(2,1)S(1)}, bf16[64,1024]{1,0:T(8,128)(2,1)S(1)}, u32[]{:S(2)}, u32[]{:S(2)}) collective-permute-start(bf16[64,1024]{1,0:T(8,128)(2,1)S(1)} %collective-permute-done.2.refs_3_), channel_id=1, source_target_pairs={{2,0},{3,1},{4,2},{5,3},{6,4},{7,5},{0,6},{1,7},{10,8},{11,9},{12,... | collective-permute-start | bytes 393224 | tf_op jit(solution)/shard_map/ppermute | solution.py:319
  16.9 6.7 %collective-permute-start.8 = (bf16[64,1024]{1,0:T(8,128)(2,1)S(1)}, bf16[64,1024]{1,0:T(8,128)(2,1)S(1)}, u32[]{:S(2)}, u32[]{:S(2)}) collective-permute-start(bf16[64,1024]{1,0:T(8,128)(2,1)S(1)} %join.6), channel_id=1, source_target_pairs={{0,8},{8,0},{16,24},{24,16},{1,9},{9,1},{17,25},{25,17},{2,10},{10... | collective-permute-start | bytes 393224 | tf_op jit(solution)/shard_map/ppermute | solution.py:343
  18.5 0.9 %copy-start = (bf16[128,1024]{1,0:T(8,128)(2,1)S(1)}, bf16[128,1024]{1,0:T(8,128)(2,1)}, u32[]{:S(2)}) copy-start(bf16[128,1024]{1,0:T(8,128)(2,1)} %get-tuple-element.10.block_hbm) | copy-start | bytes 786436
  19.4 0.7 %copy-start.1 = (s32[1024]{0:T(1024)S(1)}, s32[1024]{0:T(1024)}, u32[]{:S(2)}) copy-start(s32[1024]{0:T(1024)} %param.7) | copy-start | bytes 12292
  20.1 0.7 %copy-start.2 = (f32[1,64]{1,0:T(1,128)S(1)}, f32[1,64]{1,0:T(1,128)}, u32[]{:S(2)}) copy-start(f32[1,64]{1,0:T(1,128)} %scale_hbm.1) | copy-start | bytes 772
  21.4 17.6 %collective-permute-start.3 = (bf16[256,1024]{1,0:T(8,128)(2,1)S(1)}, bf16[256,1024]{1,0:T(8,128)(2,1)S(1)}, u32[]{:S(2)}, u32[]{:S(2)}) collective-permute-start(bf16[256,1024]{1,0:T(8,128)(2,1)S(1)} %join.4.own_ref.rest_0_), channel_id=1, source_target_pairs={{0,1},{1,0},{2,3},{3,2},{4,5},{5,4},{6,7},{7,6},{8,9},{9,8},{10,11... | collective-permute-start | bytes 1572872 | tf_op jit(solution)/shard_map/ppermute | solution.py:329
  21.5 9.2 %collective-permute-start.6 = (bf16[128,1024]{1,0:T(8,128)(2,1)S(1)}, bf16[128,1024]{1,0:T(8,128)(2,1)S(1)}, u32[]{:S(2)}, u32[]{:S(2)}) collective-permute-start(bf16[128,1024]{1,0:T(8,128)(2,1)S(1)} %join.5.rest_0_), channel_id=1, source_target_pairs={{2,0},{3,1},{4,2},{5,3},{6,4},{7,5},{0,6},{1,7},{10,8},{11,9},{12,... | collective-permute-start | bytes 786440 | tf_op jit(solution)/shard_map/ppermute | solution.py:319
  23.6 12.3 %collective-permute-start.10 = (bf16[128,1024]{1,0:T(8,128)(2,1)S(1)}, bf16[128,1024]{1,0:T(8,128)(2,1)S(1)}, u32[]{:S(2)}, u32[]{:S(2)}) collective-permute-start(bf16[128,1024]{1,0:T(8,128)(2,1)S(1)} %join.7.rest_1_), channel_id=1, source_target_pairs={{2,0},{3,1},{4,2},{5,3},{6,4},{7,5},{0,6},{1,7},{10,8},{11,9},{12,... | collective-permute-start | bytes 786440 | tf_op jit(solution)/shard_map/ppermute | solution.py:319
  24.6 16.3 %collective-permute-start.15 = (bf16[128,1024]{1,0:T(8,128)(2,1)S(1)}, bf16[128,1024]{1,0:T(8,128)(2,1)S(1)}, u32[]{:S(2)}, u32[]{:S(2)}) collective-permute-start(bf16[128,1024]{1,0:T(8,128)(2,1)S(1)} %join.5.rest_0_), channel_id=1, source_target_pairs={{0,1},{1,0},{2,3},{3,2},{4,5},{5,4},{6,7},{7,6},{8,9},{9,8},{10,11... | collective-permute-start | bytes 786440 | tf_op jit(solution)/shard_map/ppermute | solution.py:329
  24.6 19.0 %collective-permute-start.16 = (bf16[128,1024]{1,0:T(8,128)(2,1)S(1)}, bf16[128,1024]{1,0:T(8,128)(2,1)S(1)}, u32[]{:S(2)}, u32[]{:S(2)}) collective-permute-start(bf16[128,1024]{1,0:T(8,128)(2,1)S(1)} %join.7.rest_1_), channel_id=1, source_target_pairs={{0,1},{1,0},{2,3},{3,2},{4,5},{5,4},{6,7},{7,6},{8,9},{9,8},{10,11... | collective-permute-start | bytes 786440 | tf_op jit(solution)/shard_map/ppermute | solution.py:329
  30.8 18.4 %collective-permute-start.7 = (bf16[128,1024]{1,0:T(8,128)(2,1)S(1)}, bf16[128,1024]{1,0:T(8,128)(2,1)S(1)}, u32[]{:S(2)}, u32[]{:S(2)}) collective-permute-start(bf16[128,1024]{1,0:T(8,128)(2,1)S(1)} %collective-permute-done.6.rest_0_), channel_id=1, source_target_pairs={{0,1},{1,0},{2,3},{3,2},{4,5},{5,4},{6,7},{7,6},{8,9},{9,8},{10,11... | collective-permute-start | bytes 786440 | tf_op jit(solution)/shard_map/ppermute | solution.py:329
  35.9 13.2 %collective-permute-start.11 = (bf16[128,1024]{1,0:T(8,128)(2,1)S(1)}, bf16[128,1024]{1,0:T(8,128)(2,1)S(1)}, u32[]{:S(2)}, u32[]{:S(2)}) collective-permute-start(bf16[128,1024]{1,0:T(8,128)(2,1)S(1)} %collective-permute-done.10.rest_1_), channel_id=1, source_target_pairs={{0,1},{1,0},{2,3},{3,2},{4,5},{5,4},{6,7},{7,6},{8,9},{9,8},{10,11... | collective-permute-start | bytes 786440 | tf_op jit(solution)/shard_map/ppermute | solution.py:329
  39.2 9.9 %collective-permute-start.12 = (f32[8,128]{1,0:T(8,128)S(1)}, f32[8,128]{1,0:T(8,128)S(1)}, u32[]{:S(2)}, u32[]{:S(2)}) collective-permute-start(f32[8,128]{1,0:T(8,128)S(1)} %chip_trace.1.rest_5_), channel_id=1, source_target_pairs={{0,2},{1,3},{2,0},{3,1},{4,6},{5,7},{6,4},{7,5},{8,10},{9,11},{10,... | collective-permute-start | bytes 12296 | tf_op jit(solution)/shard_map/ppermute | solution.py:325
  40.8 8.3 %collective-permute-start.13 = (f32[8,128]{1,0:T(8,128)S(1)}, f32[8,128]{1,0:T(8,128)S(1)}, u32[]{:S(2)}, u32[]{:S(2)}) collective-permute-start(f32[8,128]{1,0:T(8,128)S(1)} %chip_trace.1.rest_5_), channel_id=1, source_target_pairs={{0,4},{1,5},{2,6},{3,7},{4,0},{5,1},{6,2},{7,3},{8,12},{9,13},{10,... | collective-permute-start | bytes 12296 | tf_op jit(solution)/shard_map/ppermute | solution.py:325
  43.6 5.5 %collective-permute-start.14 = (f32[8,128]{1,0:T(8,128)S(1)}, f32[8,128]{1,0:T(8,128)S(1)}, u32[]{:S(2)}, u32[]{:S(2)}) collective-permute-start(f32[8,128]{1,0:T(8,128)S(1)} %chip_trace.1.rest_5_), channel_id=1, source_target_pairs={{0,6},{1,7},{2,4},{3,5},{4,2},{5,3},{6,0},{7,1},{8,14},{9,15},{10,... | collective-permute-start | bytes 12296 | tf_op jit(solution)/shard_map/ppermute | solution.py:325
